TPU v7x, 32 devices: a whole 2x2x4 slice. The times are simulated.
32 devices in a mesh: section: 2 (over y), fsdp: 4 (over x, core), replica: 4 (over z).
Axes of the slice: x: 2, y: 2, z: 4, core: 2. Of those that a mesh axis runs over, the one named last changes fastest.
Arguments:
- images: bfloat16 [4, 32, 14, 14, 512], P(None, ('fsdp', 'replica')), may hold values from -6 to 6
- cotangent: bfloat16 [4, 32, 14, 14, 512], P(None, ('fsdp', 'replica')), may hold values from -6 to 6
- counts: int32 [4, 16], P(None, ('fsdp', 'replica')), may hold values from 1 to 2, as said below
- regions: int32 [14, 14], replicated, may hold values from 0 to 8, as said below
- relpos: int32 [49, 49], replicated, may hold values from 0 to 168, as said below
- qkv_weight: bfloat16 [2, 512, 1536], P('section', 'fsdp'), may hold values from -0.25 to 0.25
- proj_weight: bfloat16 [2, 512, 512], P('section', 'fsdp'), may hold values from -1.5 to 1.5
- fc1_weight: bfloat16 [2, 512, 2048], P('section', 'fsdp'), may hold values from -0.25 to 0.25
- fc2_weight: bfloat16 [2, 2048, 512], P('section', 'fsdp'), may hold values from -0.125 to 0.125
- gains: bfloat16 [2, 2, 512], P('section', None, 'fsdp'), may hold values from 0.099609375 to 1.8984375
- biases: bfloat16 [2, 6, 512], P('section', None, 'fsdp'), may hold values from -3 to 3
- fc1_bias: bfloat16 [2, 2048], P('section', 'fsdp'), may hold values from -3 to 3
- rel_table: bfloat16 [2, 169, 16], P('section', None, 'fsdp'), may hold values from -5 to 5
Outputs:
- block_out: bfloat16 [2, 4, 32, 14, 14, 512], P('section', None, ('fsdp', 'replica'))
- input_grad: float32 [2, 4, 32, 14, 14, 512], P('section', None, ('fsdp', 'replica'))
- grad_qkv: float32 [2, 512, 1536], P('section', 'fsdp')
- grad_proj: float32 [2, 512, 512], P('section', 'fsdp')
- grad_fc1: float32 [2, 512, 2048], P('section', 'fsdp')
- grad_fc2: float32 [2, 2048, 512], P('section', 'fsdp')
- grad_gains: float32 [2, 2, 512], P('section', None, 'fsdp')
- grad_biases: float32 [2, 6, 512], P('section', None, 'fsdp')
- grad_fc1_bias: float32 [2, 2048], P('section', 'fsdp')
- grad_table: float32 [2, 169, 16], P('section', None, 'fsdp')
Inputs may be any that keep to these rules, and one draw needn't show every extreme that they name: `counts`: slots 0 to count - 1 of a device's 2 slots in a micro-batch are live; in every micro-batch some device has all 2 live. `regions`: region ids are constant on bands: id = 3 * band(row) + band(column) with the same two cut positions for rows and columns. `relpos`: pairs with the same relative offset share a row; every row is used.
All inputs are finite; a program needn't handle non-finite values.
Results may differ from a plain program's by a relative error of at most 0.019.
Values may be sent and summed in bfloat16 or wider, within the bound.
No kernel may reach another device: no remote copies, remote signals or barrier semaphores. Data moves between devices by JAX's collectives and lax.ppermute only.
A program may use at most 320 MiB of HBM per device.

v0:
```python
import jax
import jax.numpy as jnp
from jax import lax
from jax.sharding import PartitionSpec as P

DIM = 512
HEADS = 16
HEAD_DIM = 32
WIN = 7
SIDE = 14
SHIFT = 3
TABLE = 169
EPSILON = 1e-05
ROOT_HALF = 0.7071067811865476
INV_ROOT_TAU = 0.3989422804014327


def shifted(value, axis, by):
    length = lax.axis_size(axis)
    pairs = [(i, i + by) for i in range(length) if 0 <= i + by < length]
    return lax.ppermute(value, axis, pairs)


def layer_norm(values, gain, offset_row):
    center = values - jnp.mean(values, axis=-1, keepdims=True)
    spread = jnp.mean(center * center, axis=-1, keepdims=True)
    scaled = lax.rsqrt(spread + EPSILON)
    normed = center * scaled
    return (normed * gain + offset_row, normed, scaled)


def norm_backward(upstream, normed, scaled, gain):
    direct = upstream * gain
    return (
        direct
        - jnp.mean(direct, axis=-1, keepdims=True)
        - normed * jnp.mean(direct * normed, axis=-1, keepdims=True)
    ) * scaled


def gelu_value(before):
    return 0.5 * before * (1.0 + jax.scipy.special.erf(before * ROOT_HALF))


def gelu_slope(before):
    return 0.5 * (
        1.0 + jax.scipy.special.erf(before * ROOT_HALF)
    ) + before * INV_ROOT_TAU * jnp.exp(-0.5 * before * before)


def inner_rows(left, right):
    return lax.dot_general(
        left, right, (((0,), (0,)), ((), ())), preferred_element_type=jnp.float32
    )


def outer_cols(left, right):
    return lax.dot_general(
        left, right, (((1,), (1,)), ((), ())), preferred_element_type=jnp.float32
    )


def to_windows(image_rows, offset):
    rolled = jnp.roll(image_rows, (-offset, -offset), axis=(1, 2))
    count = image_rows.shape[0]
    parts = SIDE // WIN
    shaped = rolled.reshape(count, parts, WIN, parts, WIN, DIM).transpose(0, 1, 3, 2, 4, 5)
    return shaped.reshape(count * SIDE * SIDE, DIM)


def from_windows(window_rows, offset):
    count = window_rows.shape[0] // (SIDE * SIDE)
    parts = SIDE // WIN
    shaped = window_rows.reshape(count, parts, parts, WIN, WIN, DIM).transpose(0, 1, 3, 2, 4, 5)
    return jnp.roll(shaped.reshape(count, SIDE, SIDE, DIM), (offset, offset), axis=(1, 2))


def relation_onehot(relpos):
    flat = relpos.reshape(-1)
    return (flat[:, None] == jnp.arange(TABLE, dtype=jnp.int32)[None, :]).astype(jnp.float32)


def region_mask(regions, later):
    parts = SIDE // WIN
    tiles = (
        regions.reshape(parts, WIN, parts, WIN)
        .transpose(0, 2, 1, 3)
        .reshape(parts * parts, WIN * WIN)
    )
    differ = (tiles[:, :, None] != tiles[:, None, :]) & later
    return jnp.where(differ, jnp.float32(-100.0), jnp.float32(0.0))


def window_eye():
    count = (SIDE // WIN) ** 2
    return lax.broadcasted_iota(jnp.int32, (count, count), 0) == lax.broadcasted_iota(
        jnp.int32, (count, count), 1
    )


def attention_add(table, onehot, masking):
    lookup = jnp.dot(onehot, table.astype(jnp.float32), precision=lax.Precision.HIGHEST)
    lookup = lookup.reshape(WIN * WIN, WIN * WIN, HEADS).transpose(2, 0, 1)
    windowed = lookup[None] + masking[:, None]
    count = (SIDE // WIN) ** 2
    eye = window_eye()
    spread_add = jnp.where(
        eye[None, :, None, :, None],
        windowed.transpose(1, 0, 2, 3)[:, :, :, None, :],
        jnp.float32(0.0),
    )
    full_add = spread_add.reshape(HEADS, count * WIN * WIN, count * WIN * WIN)
    same = jnp.broadcast_to(eye[:, None, :, None], (count, WIN * WIN, count, WIN * WIN)).reshape(
        count * WIN * WIN, count * WIN * WIN
    )
    return (full_add, same)


def forward(rows, params, added):
    qkv_w, proj_w, fc1_w, fc2_w, gain_rows, bias_rows, fc1_b, table = params
    full_add, same = added
    gains_f = gain_rows.astype(jnp.float32)
    biases_f = bias_rows.astype(jnp.float32)
    factor = HEAD_DIM ** (-0.5)
    base = rows.astype(jnp.float32)
    first, normed_a, scaled_a = layer_norm(base, gains_f[0], biases_f[0])
    first_b = first.astype(jnp.bfloat16)
    mixed = jnp.dot(first_b, qkv_w, preferred_element_type=jnp.float32)
    count = rows.shape[0] // (SIDE * SIDE)
    blocks = (count, SIDE * SIDE, HEADS, HEAD_DIM)
    query_blocks = ((mixed[:, :DIM] + biases_f[1]) * factor).astype(jnp.bfloat16).reshape(blocks)
    key_blocks = mixed[:, DIM : 2 * DIM].astype(jnp.bfloat16).reshape(blocks)
    value_blocks = (mixed[:, 2 * DIM :] + biases_f[2]).astype(jnp.bfloat16).reshape(blocks)
    scores = (
        jnp.einsum("sihd,sjhd->shij", query_blocks, key_blocks, preferred_element_type=jnp.float32)
        + full_add[None]
    )
    expo = jnp.where(same[None, None], jnp.exp(scores), jnp.float32(0.0))
    probs = expo / jnp.sum(expo, axis=-1, keepdims=True)
    probs_b = probs.astype(jnp.bfloat16)
    attended = jnp.einsum(
        "shij,sjhd->sihd", probs_b, value_blocks, preferred_element_type=jnp.float32
    )
    attended = attended.astype(jnp.bfloat16).reshape(rows.shape[0], DIM)
    middle = base + jnp.dot(attended, proj_w, preferred_element_type=jnp.float32) + biases_f[3]
    second, normed_b, scaled_b = layer_norm(middle, gains_f[1], biases_f[4])
    second_b = second.astype(jnp.bfloat16)
    before = jnp.dot(second_b, fc1_w, preferred_element_type=jnp.float32) + fc1_b.astype(
        jnp.float32
    )
    hidden_b = gelu_value(before).astype(jnp.bfloat16)
    output = middle + jnp.dot(hidden_b, fc2_w, preferred_element_type=jnp.float32) + biases_f[5]
    saved = (
        normed_a,
        scaled_a,
        first_b,
        query_blocks,
        key_blocks,
        value_blocks,
        probs,
        probs_b,
        attended,
        normed_b,
        scaled_b,
        second_b,
        before,
        hidden_b,
    )
    return (output.astype(jnp.bfloat16), saved)


def backward(upstream_rows, saved, params, onehot):
    qkv_w, proj_w, fc1_w, fc2_w, gain_rows, bias_rows, fc1_b, table = params
    gains_f = gain_rows.astype(jnp.float32)
    factor = HEAD_DIM ** (-0.5)
    (
        normed_a,
        scaled_a,
        first_b,
        query_blocks,
        key_blocks,
        value_blocks,
        probs,
        probs_b,
        attended,
        normed_b,
        scaled_b,
        second_b,
        before,
        hidden_b,
    ) = saved
    upstream = upstream_rows.astype(jnp.float32)
    grad_fc2_bias = jnp.sum(upstream, axis=0)
    grad_fc2 = inner_rows(hidden_b, upstream_rows)
    grad_before = outer_cols(upstream_rows, fc2_w) * gelu_slope(before)
    grad_before_b = grad_before.astype(jnp.bfloat16)
    grad_fc1_bias = jnp.sum(grad_before, axis=0)
    grad_fc1 = inner_rows(second_b, grad_before_b)
    grad_second = outer_cols(grad_before_b, fc1_w)
    grad_gain_b = jnp.sum(grad_second * normed_b, axis=0)
    grad_shift_b = jnp.sum(grad_second, axis=0)
    grad_middle = upstream + norm_backward(grad_second, normed_b, scaled_b, gains_f[1])
    grad_middle_b = grad_middle.astype(jnp.bfloat16)
    grad_proj_bias = jnp.sum(grad_middle, axis=0)
    grad_proj = inner_rows(attended, grad_middle_b)
    grad_attended = (
        outer_cols(grad_middle_b, proj_w).astype(jnp.bfloat16).reshape(query_blocks.shape)
    )
    grad_probs = jnp.einsum(
        "sihd,sjhd->shij", grad_attended, value_blocks, preferred_element_type=jnp.float32
    )
    grad_scores = probs * (grad_probs - jnp.sum(probs * grad_probs, axis=-1, keepdims=True))
    grad_scores_b = grad_scores.astype(jnp.bfloat16)
    count = (SIDE // WIN) ** 2
    summed = jnp.sum(grad_scores, axis=0).reshape(HEADS, count, WIN * WIN, count, WIN * WIN)
    eye_f = window_eye().astype(jnp.float32)
    table_terms = jnp.einsum(
        "hwivj,wv->ijh", summed, eye_f, precision=lax.Precision.HIGHEST
    ).reshape(WIN**4, HEADS)
    grad_table = lax.dot_general(
        onehot, table_terms, (((0,), (0,)), ((), ())), precision=lax.Precision.HIGHEST
    )
    total_rows = first_b.shape[0]
    grad_queries = (
        jnp.einsum("shij,sjhd->sihd", grad_scores_b, key_blocks, preferred_element_type=jnp.float32)
        * factor
    ).reshape(total_rows, DIM)
    grad_keys = jnp.einsum(
        "shij,sihd->sjhd", grad_scores_b, query_blocks, preferred_element_type=jnp.float32
    ).reshape(total_rows, DIM)
    grad_values = jnp.einsum(
        "shij,sihd->sjhd", probs_b, grad_attended, preferred_element_type=jnp.float32
    ).reshape(total_rows, DIM)
    grad_mixed_b = jnp.concatenate([grad_queries, grad_keys, grad_values], axis=1).astype(
        jnp.bfloat16
    )
    grad_qkv = inner_rows(first_b, grad_mixed_b)
    grad_first = outer_cols(grad_mixed_b, qkv_w)
    grad_gain_a = jnp.sum(grad_first * normed_a, axis=0)
    grad_shift_a = jnp.sum(grad_first, axis=0)
    grad_rows = grad_middle + norm_backward(grad_first, normed_a, scaled_a, gains_f[0])
    grad_gains = jnp.stack([grad_gain_a, grad_gain_b])
    grad_biases = jnp.stack(
        [
            grad_shift_a,
            jnp.sum(grad_queries, axis=0),
            jnp.sum(grad_values, axis=0),
            grad_proj_bias,
            grad_shift_b,
            grad_fc2_bias,
        ]
    )
    return (
        grad_rows,
        (
            grad_qkv,
            grad_proj,
            grad_fc1,
            grad_fc2,
            grad_gains,
            grad_biases,
            grad_fc1_bias,
            grad_table,
        ),
    )


def keep_slot(store, fresh, place, valid):
    former = lax.dynamic_index_in_dim(store, place, 0, keepdims=False)
    return lax.dynamic_update_index_in_dim(store, jnp.where(valid, fresh, former), place, 0)


def add_trees(left, right):
    if left is None:
        return right
    return jax.tree.map(lambda first, second: first + second, left, right)


def shards(
    images,
    cotangent,
    counts,
    regions,
    relpos,
    qkv_weight,
    proj_weight,
    fc1_weight,
    fc2_weight,
    gains,
    biases,
    fc1_bias,
    rel_table,
):
    section = lax.axis_index("section")
    later = section == 1
    offset = SHIFT * section
    micro = images.shape[0]
    slots = images.shape[1]
    live = lax.broadcasted_iota(jnp.int32, (micro, slots), 1) < counts
    onehot = relation_onehot(relpos)
    masking = region_mask(regions, later)
    zero_half = jnp.zeros((), jnp.bfloat16)
    held = (
        lax.all_gather(qkv_weight[0], "fsdp", axis=0, tiled=True),
        lax.all_gather(proj_weight[0], "fsdp", axis=0, tiled=True),
        lax.all_gather(fc1_weight[0], "fsdp", axis=0, tiled=True),
        lax.all_gather(fc2_weight[0], "fsdp", axis=0, tiled=True),
        lax.all_gather(gains[0], "fsdp", axis=1, tiled=True),
        lax.all_gather(biases[0], "fsdp", axis=1, tiled=True),
        lax.all_gather(fc1_bias[0], "fsdp", axis=0, tiled=True),
        lax.all_gather(rel_table[0], "fsdp", axis=1, tiled=True),
    )

    def fetch():
        return held

    carried = jnp.zeros(images.shape[1:], jnp.bfloat16)
    inputs_kept = jnp.zeros_like(images)
    outputs = jnp.zeros_like(images)
    for moment in range(micro + 1):
        position = moment - section
        valid = (position >= 0) & (position < micro)
        place = jnp.clip(position, 0, micro - 1)
        source = jnp.where(later, carried, images[min(moment, micro - 1)])
        params = fetch()
        added = attention_add(params[7], onehot, masking)
        result_rows, unused = forward(to_windows(source, offset), params, added)
        alive = lax.dynamic_index_in_dim(live, place, 0, keepdims=False)[:, None, None, None]
        result = jnp.where(alive, from_windows(result_rows, offset), zero_half)
        inputs_kept = keep_slot(inputs_kept, source, place, valid)
        outputs = keep_slot(outputs, result, place, valid)
        if moment < micro:
            carried = shifted(result, "section", 1)
    returned = jnp.zeros(images.shape[1:], jnp.bfloat16)
    input_grads = jnp.zeros(images.shape, jnp.float32)
    totals = None
    for moment in range(micro + 1):
        position = moment - 1 + section
        valid = (position >= 0) & (position < micro)
        place = jnp.clip(position, 0, micro - 1)
        alive = lax.dynamic_index_in_dim(live, place, 0, keepdims=False)[:, None, None, None]
        incoming = jnp.where(later, cotangent[min(moment, micro - 1)], returned)
        incoming = jnp.where(valid & alive, incoming, zero_half)
        source = lax.dynamic_index_in_dim(inputs_kept, place, 0, keepdims=False)
        params = fetch()
        added = attention_add(params[7], onehot, masking)
        unused, saved = forward(to_windows(source, offset), params, added)
        grad_rows, terms = backward(to_windows(incoming, offset), saved, params, onehot)
        grad_input = from_windows(grad_rows, offset)
        input_grads = keep_slot(input_grads, grad_input, place, valid)
        totals = add_trees(totals, terms)
        if moment < micro:
            returned = shifted(grad_input.astype(jnp.bfloat16), "section", -1)
    parted = (
        lax.psum_scatter(
            totals[0].astype(jnp.bfloat16), "fsdp", scatter_dimension=0, tiled=True
        ).astype(jnp.float32),
        lax.psum_scatter(
            totals[1].astype(jnp.bfloat16), "fsdp", scatter_dimension=0, tiled=True
        ).astype(jnp.float32),
        lax.psum_scatter(
            totals[2].astype(jnp.bfloat16), "fsdp", scatter_dimension=0, tiled=True
        ).astype(jnp.float32),
        lax.psum_scatter(
            totals[3].astype(jnp.bfloat16), "fsdp", scatter_dimension=0, tiled=True
        ).astype(jnp.float32),
        lax.psum_scatter(
            totals[4].astype(jnp.bfloat16), "fsdp", scatter_dimension=1, tiled=True
        ).astype(jnp.float32),
        lax.psum_scatter(
            totals[5].astype(jnp.bfloat16), "fsdp", scatter_dimension=1, tiled=True
        ).astype(jnp.float32),
        lax.psum_scatter(
            totals[6].astype(jnp.bfloat16), "fsdp", scatter_dimension=0, tiled=True
        ).astype(jnp.float32),
        lax.psum_scatter(
            totals[7].astype(jnp.bfloat16), "fsdp", scatter_dimension=1, tiled=True
        ).astype(jnp.float32),
    )
    shares = (
        lax.psum(parted[0].astype(jnp.bfloat16), "replica").astype(jnp.float32),
        lax.psum(parted[1].astype(jnp.bfloat16), "replica").astype(jnp.float32),
        lax.psum(parted[2].astype(jnp.bfloat16), "replica").astype(jnp.float32),
        lax.psum(parted[3].astype(jnp.bfloat16), "replica").astype(jnp.float32),
        lax.psum(parted[4].astype(jnp.bfloat16), "replica").astype(jnp.float32),
        lax.psum(parted[5].astype(jnp.bfloat16), "replica").astype(jnp.float32),
        lax.psum(parted[6].astype(jnp.bfloat16), "replica").astype(jnp.float32),
        lax.psum(parted[7].astype(jnp.bfloat16), "replica").astype(jnp.float32),
    )
    return (
        outputs[None],
        input_grads[None],
        shares[0][None],
        shares[1][None],
        shares[2][None],
        shares[3][None],
        shares[4][None],
        shares[5][None],
        shares[6][None],
        shares[7][None],
    )


def solution(mesh):
    in_specs = (
        P(None, ("fsdp", "replica"), None, None, None),
        P(None, ("fsdp", "replica"), None, None, None),
        P(None, ("fsdp", "replica")),
        P(),
        P(),
        P("section", "fsdp", None),
        P("section", "fsdp", None),
        P("section", "fsdp", None),
        P("section", "fsdp", None),
        P("section", None, "fsdp"),
        P("section", None, "fsdp"),
        P("section", "fsdp"),
        P("section", None, "fsdp"),
    )
    out_specs = (
        P("section", None, ("fsdp", "replica"), None, None, None),
        P("section", None, ("fsdp", "replica"), None, None, None),
        P("section", "fsdp", None),
        P("section", "fsdp", None),
        P("section", "fsdp", None),
        P("section", "fsdp", None),
        P("section", None, "fsdp"),
        P("section", None, "fsdp"),
        P("section", "fsdp"),
        P("section", None, "fsdp"),
    )
    return jax.shard_map(shards, mesh=mesh, in_specs=in_specs, out_specs=out_specs, check_vma=False)
```

profile of v0, /device:TPU:0, one launch (start us, length us, event | category | flops | bytes accessed | tf_op | source)
XLA Modules:
  0.0 1292.6 jit_solution(11657054412358554816)
XLA Ops:
  48.0 10.8 all-gather.4
  116.6 11.8 fusion.474
  520.8 16.6 %fusion.14 = (f32[2,16,196]{2,1,0:T(8,128)S(1)}, f32[2,16,196]{2,1,0:T(8,128)}, f32[2,16,196]{2,1,0:T(8,128)S(1)}, f32[2,16,196]{2,1,0:T(8,128)S(1)}, f32[2,16,1...) fusion(f32[16,196,196]{1,2,0:T(8,128)S(1)} %copy.870, ...), kind=kOutput, calls=%fused_computation.39 | convolution fusion | flops 100765952 | bytes 32953872 | tf_op jit(solution)/shard_map/sihd,sjhd->shij/dot_general | solution.py:135
  537.4 19.7 %fusion.13 = (f32[2,16,196,196]{2,3,1,0:T(8,128)}, f32[2,16,196,196]{2,3,1,0:T(8,128)S(1)}, f32[2,16,196,196]{2,3,1,0:T(8,128)}, f32[2,16,196,196]{2,3,1,0:T(8,128)}, f32[2,16,196,196]{2,3,1,0:T(8,128)}) fusion(f32[2,16,196,196]{2,3,1,0:T(8,128)} %get-tuple-element.238, f32[2,16,196]{2,1,0:T(8,128)S(1)} %get-tuple-element.42, f32[16,196,196]{1,2,0:T(8,128)S(1)} %copy.870, ...), kind=kLoop, calls=%fused_computation.38 | loop fusion | flops 18439680 | bytes 51794960 | tf_op jit(solution)/shard_map/div | solution.py:139
  591.2 8.1 fusion.41
  752.0 7.6 fusion.43
  812.5 7.0 multiply_reduce_fusion.2
  819.5 7.6 fusion.45
  878.2 7.0 multiply_reduce_fusion.1
  885.2 7.6 fusion.47
  950.1 7.7 fusion.49
  1012.1 12.7 copy.1077
  1024.9 8.1 fusion.661
  1050.5 13.1 %copy.1079 = f32[16,4,49,4,49]{4,3,1,2,0:T(4,128)} copy(f32[16,4,49,4,49]{2,1,4,3,0:T(4,128)} %reshape.1264) | data formatting | bytes 4917248 | tf_op jit(solution)/shard_map/reshape | solution.py:215
  1075.0 8.0 fusion.662
  1097.9 12.7 copy.1081
  1110.7 8.0 fusion.663
  1135.6 12.9 copy.1083
  1148.6 8.1 fusion.664
  1177.8 12.7 copy.1085
  1190.6 8.2 fusion.665
  1200.9 10.1 all-reduce.4
  1216.7 12.9 all-reduce.2
  1231.9 46.6 %all-reduce.7.cloned.1.call-done = (bf16[1,128,1536]{2,1,0:T(8,128)(2,1)}, bf16[1,128,512]{2,1,0:T(8,128)(2,1)}, bf16[1,128,2048]{2,1,0:T(8,128)(2,1)}, bf16[1,512,512]{2,1,0:T(8,128)(2,1)}) async-done(((bf16[1,128,1536]{2,1,0:T(8,128)(2,1)}, bf16[1,128,512]{2,1,0:T(8,128)(2,1)}, bf16[1,128,2048]{2,1,0:T(8,128)(2,1)}, bf16[1,512,512]{2,1,0:T(8,128)(2,1)}), (bf16[1,128,1536]{2,1,0:T(8,128)(2,1)}, ...) | async-done | bytes 1572880 | tf_op jit(solution)/shard_map/psum | solution.py:381
  (1189 shorter events, 987.8 us)
Async XLA Ops:
  7.2 66.3 %all-gather.12.cloned.1.call-start = ((), (), s32[]{:S(2)}) async-start(), calls=%async_computation.10 | async-start | bytes 1966080 | tf_op jit(solution)/shard_map/all_gather | solution.py:304
  7.9 96.7 %all-gather.16.cloned.1.call-start = ((), (), s32[]{:S(2)}) async-start(), calls=%async_computation.12 | async-start | bytes 2621440 | tf_op jit(solution)/shard_map/all_gather | solution.py:307
  8.7 96.0 %all-gather.14.cloned.1.call-start = ((), (), s32[]{:S(2)}) async-start(), calls=%async_computation.11 | async-start | bytes 2621440 | tf_op jit(solution)/shard_map/all_gather | solution.py:306
  9.4 1155.6 %reduce-scatter.13.cloned.1.call-start = ((), (), s32[]{:S(2)}) async-start(), calls=%async_computation.7 | async-start | bytes 655360 | tf_op jit(solution)/shard_map/reduce_scatter | solution.py:358
  15.9 265.0 %copy-start.180 = (f32[1,1,512]{2,1,0:T(1,128)}, f32[1,1,512]{2,1,0:T(1,128)S(1)}, u32[]{:S(2)}) copy-start(f32[1,1,512]{2,1,0:T(1,128)S(1)} %get-tuple-element.197) | copy-start | bytes 6148
  15.9 265.0 %copy-start.182 = (f32[1,1,512]{2,1,0:T(1,128)}, f32[1,1,512]{2,1,0:T(1,128)S(1)}, u32[]{:S(2)}) copy-start(f32[1,1,512]{2,1,0:T(1,128)S(1)} %get-tuple-element.198) | copy-start | bytes 6148
  15.9 289.9 %copy-start.191 = (f32[1,1,512]{2,1,0:T(1,128)}, f32[1,1,512]{2,1,0:T(1,128)S(1)}, u32[]{:S(2)}) copy-start(f32[1,1,512]{2,1,0:T(1,128)S(1)} %get-tuple-element.194) | copy-start | bytes 6148
  15.9 289.9 %copy-start.221 = (f32[1,1,512]{2,1,0:T(1,128)}, f32[1,1,512]{2,1,0:T(1,128)S(1)}, u32[]{:S(2)}) copy-start(f32[1,1,512]{2,1,0:T(1,128)S(1)} %get-tuple-element.195) | copy-start | bytes 6148
  15.9 689.0 %copy-start.158 = (f32[1,1,512]{2,1,0:T(1,128)}, f32[1,1,512]{2,1,0:T(1,128)S(1)}, u32[]{:S(2)}) copy-start(f32[1,1,512]{2,1,0:T(1,128)S(1)} %get-tuple-element.196) | copy-start | bytes 6148
  46.0 259.8 %copy-start.177 = (f32[1,1,512]{2,1,0:T(1,128)}, f32[1,1,512]{2,1,0:T(1,128)S(1)}, u32[]{:S(2)}) copy-start(f32[1,1,512]{2,1,0:T(1,128)S(1)} %get-tuple-element.210) | copy-start | bytes 6148
  128.4 12.7 collective-permute-start
  192.4 12.9 collective-permute-start.1
  256.4 12.0 collective-permute-start.2
  319.6 12.5 collective-permute-start.3
  662.8 64.1 %collective-permute-start.4 = (bf16[2,14,14,512]{3,0,2,1:T(2,128)(2,1)}, bf16[2,14,14,512]{3,0,2,1:T(2,128)(2,1)}, u32[]{:S(2)}, u32[]{:S(2)}) collective-permute-start(bf16[2,14,14,512]{3,0,2,1:T(2,128)(2,1)} %get-tuple-element.114), channel_id=1, source_target_pairs={{16,0},{17,1},{18,2},{19,3},{20,4},{21,5},{22,6},{23,7},{24,8},{25... | collective-permute-start | bytes 1204232 | tf_op jit(solution)/shard_map/ppermute | solution.py:21
  784.9 11.2 collective-permute-start.5
  852.6 9.7 collective-permute-start.6
  918.2 9.7 collective-permute-start.7
  972.3 192.7 %reduce-scatter.11.cloned.1.call-start = ((), (), s32[]{:S(2)}) async-start(), calls=%async_computation.6 | async-start | bytes 1966080 | tf_op jit(solution)/shard_map/reduce_scatter | solution.py:355
  984.9 180.1 %reduce-scatter.15.cloned.1.call-start = ((), (), s32[]{:S(2)}) async-start(), calls=%async_computation.8 | async-start | bytes 2621440 | tf_op jit(solution)/shard_map/reduce_scatter | solution.py:361
  997.0 168.1 %reduce-scatter.17.cloned.1.call-start = ((), (), s32[]{:S(2)}) async-start(), calls=%async_computation.9 | async-start | bytes 2621440 | tf_op jit(solution)/shard_map/reduce_scatter | solution.py:364
  1075.0 140.1 %reduce-scatter.19.cloned.1.call-start = ((), (), s32[]{:S(2)}) async-start(), calls=%async_computation.13 | async-start | bytes 163840
  1164.0 51.9 %reduce-scatter.21.cloned.1.call-start = ((), (), s32[]{:S(2)}) async-start(), calls=%async_computation.14 | async-start | bytes 163840
  1164.9 113.6 %all-reduce.7.cloned.1.call-start = ((), (), s32[]{:S(2)}) async-start(), calls=%async_computation.15 | async-start | bytes 3145728 | tf_op jit(solution)/shard_map/psum | solution.py:381
  (256 other events, 1883.9 us)
Sparse Core Ops, SparseCore 0:
  9.6 22.4 all-gather.11
  33.6 23.9 all-gather.15
  59.2 22.3 all-gather.13
  972.4 20.7 reduce-scatter.12
  995.6 28.0 reduce-scatter.10
  1026.1 31.1 reduce-scatter.14
  1075.1 31.0 reduce-scatter.16
  1164.1 19.4 reduce-scatter.18
  1186.6 19.7 reduce-scatter.20
  1208.8 69.6 all-reduce.6
where the time goes:
time: 1310 us; the launch traced here: 1290 us
  local copies, waits for them, and re-layouts  503 us (38%)
  matrix products  377 us (29%)
  other arithmetic  239 us (18%)
  waiting for transfers between devices  73.6 us (6%)
  blocking collectives  56.6 us (4%)
  starting transfers between devices  24.5 us (2%)
  between operations  19.3 us (1%)
    reshape x10, local copies, waits for them, and re-layouts, backward(): jnp.sum(grad_scores, axis=0)  93.8 us
    dot_general x10, matrix products, forward(): jnp.einsum('sihd,sjhd->shij', query_blocks, key_blocks, preferred_element...  49.7 us
    dot_general x20, matrix products, outer_cols(): lax.dot_general(left, right, (((1,), (1,)), ((), ())), preferred_element_...  49.6 us
    dot_general x20, matrix products, inner_rows(): lax.dot_general(left, right, (((0,), (0,)), ((), ())), preferred_element_...  47 us
    psum x1, waiting for transfers between devices, shards(): lax.psum(parted[0].astype(jnp.bfloat16), 'replica').astype(jnp.float32)  46.6 us
    dynamic_update_slice x15, other arithmetic, keep_slot(): lax.dynamic_update_index_in_dim(store, jnp.where(valid, fresh, former), p...  46.5 us
    unnamed x544, local copies, waits for them, and re-layouts  46.2 us
    dot_general x5, matrix products, backward(): jnp.einsum('hwivj,wv->ijh', summed, eye_f, precision=lax.Precision.HIGHEST)  40.3 us
  transfers between devices with their start and end apart: 18, of which 7 were waited for; matrix products, arithmetic and copies ran while one was open for 29% of the time, Pallas kernels for 0%

commit v1 on v0

--- a/solution.py
+++ b/solution.py
@@ -2,6 +2,7 @@
 import jax.numpy as jnp
 from jax import lax
 from jax.sharding import PartitionSpec as P
+from jax.lax import all_gather
 
 DIM = 512
 HEADS = 16
@@ -13,6 +14,10 @@
 EPSILON = 1e-05
 ROOT_HALF = 0.7071067811865476
 INV_ROOT_TAU = 0.3989422804014327
+
+
+def part_edges_on_mesh(z_in):
+    return jnp.sum(all_gather(z_in, "replica"), axis=0)
 
 
 def shifted(value, axis, by):
@@ -378,7 +383,7 @@
         ).astype(jnp.float32),
     )
     shares = (
-        lax.psum(parted[0].astype(jnp.bfloat16), "replica").astype(jnp.float32),
+        part_edges_on_mesh(parted[0].astype(jnp.bfloat16)).astype(jnp.float32),
         lax.psum(parted[1].astype(jnp.bfloat16), "replica").astype(jnp.float32),
         lax.psum(parted[2].astype(jnp.bfloat16), "replica").astype(jnp.float32),
         lax.psum(parted[3].astype(jnp.bfloat16), "replica").astype(jnp.float32),

time: 1310 us -> 1230 us (0.939)
  local copies, waits for them, and re-layouts: 503 us -> 463 us
  waiting for transfers between devices: 73.6 us -> 38.2 us
    psum x1, waiting for transfers between devices: 46.6 us -> 0.01 us  [shards(): lax.psum(parted[1].astype(jnp.bfloat16), 'replica').astype(jnp.float32)]
    unnamed x544 -> x534, local copies, waits for them, and re-layouts: 46.2 us -> 40.4 us
  transfers between devices with their start and end apart: 18 -> 19, of which waited for: 7 -> 7; matrix products, arithmetic and copies ran while one was open for 29% -> 33% of each run, Pallas kernels for 0% -> 0%
where the time goes in v1:
time: 1230 us; the launch traced here: 1210 us
  local copies, waits for them, and re-layouts  463 us (38%)
  matrix products  380 us (31%)
  other arithmetic  229 us (19%)
  blocking collectives  57.1 us (5%)
  waiting for transfers between devices  38.2 us (3%)
  starting transfers between devices  25.3 us (2%)
  between operations  19 us (2%)
    reshape x10, local copies, waits for them, and re-layouts, backward(): jnp.sum(grad_scores, axis=0)  96.8 us
    dot_general x20, matrix products, inner_rows(): lax.dot_general(left, right, (((0,), (0,)), ((), ())), preferred_element_...  52.6 us
    dot_general x20, matrix products, outer_cols(): lax.dot_general(left, right, (((1,), (1,)), ((), ())), preferred_element_...  50.2 us
    dot_general x10, matrix products, forward(): jnp.einsum('sihd,sjhd->shij', query_blocks, key_blocks, preferred_element...  49.3 us
    dot_general x5, matrix products, backward(): jnp.einsum('hwivj,wv->ijh', summed, eye_f, precision=lax.Precision.HIGHEST)  41.1 us
    unnamed x534, local copies, waits for them, and re-layouts  40.4 us
    concatenate x27, other arithmetic, to_windows(): rolled = jnp.roll(image_rows, (-offset, -offset), axis=(1, 2))  39 us
    reduce_sum x5, other arithmetic, backward(): jnp.sum(grad_scores, axis=0)  38.7 us
  transfers between devices with their start and end apart: 19, of which 7 were waited for; matrix products, arithmetic and copies ran while one was open for 33% of the time, Pallas kernels for 0%

profile of v1, /device:TPU:0, one launch (start us, length us, event | category | flops | bytes accessed | tf_op | source)
XLA Modules:
  0.0 1210.7 jit_solution(7831049563226637986)
XLA Ops:
  47.9 10.9 all-gather.4
  511.3 16.5 %fusion.14 = (f32[2,16,196]{2,1,0:T(8,128)S(1)}, f32[2,16,196]{2,1,0:T(8,128)}, f32[2,16,196]{2,1,0:T(8,128)S(1)}, f32[2,16,196]{2,1,0:T(8,128)S(1)}, f32[2,16,1...) fusion(f32[16,196,196]{1,2,0:T(8,128)S(1)} %copy.870, ...), kind=kOutput, calls=%fused_computation.39 | convolution fusion | flops 100765952 | bytes 32953872 | tf_op jit(solution)/shard_map/sihd,sjhd->shij/dot_general | solution.py:140
  527.8 19.7 %fusion.13 = (f32[2,16,196,196]{2,3,1,0:T(8,128)}, f32[2,16,196,196]{2,3,1,0:T(8,128)S(1)}, f32[2,16,196,196]{2,3,1,0:T(8,128)}, f32[2,16,196,196]{2,3,1,0:T(8,128)}, f32[2,16,196,196]{2,3,1,0:T(8,128)}) fusion(f32[2,16,196,196]{2,3,1,0:T(8,128)} %get-tuple-element.237, f32[2,16,196]{2,1,0:T(8,128)S(1)} %get-tuple-element.42, f32[16,196,196]{1,2,0:T(8,128)S(1)} %copy.870, ...), kind=kLoop, calls=%fused_computation.38 | loop fusion | flops 18439680 | bytes 51794960 | tf_op jit(solution)/shard_map/div | solution.py:144
  574.8 7.1 multiply_reduce_fusion.4
  581.9 8.2 fusion.41
  699.5 7.6 fusion.43
  760.6 7.0 multiply_reduce_fusion.2
  767.6 7.6 fusion.45
  832.1 7.6 fusion.47
  891.1 7.4 add_convert_fusion.1
  910.9 13.1 %copy.1077 = f32[16,4,49,4,49]{4,3,1,2,0:T(4,128)} copy(f32[16,4,49,4,49]{2,1,4,3,0:T(4,128)} %reshape.1274) | data formatting | bytes 4917248 | tf_op jit(solution)/shard_map/reshape | solution.py:220
  924.1 8.1 fusion.661
  965.9 7.7 fusion.49
  1008.1 12.8 %copy.1079 = f32[16,4,49,4,49]{4,3,1,2,0:T(4,128)} copy(f32[16,4,49,4,49]{2,1,4,3,0:T(4,128)} %reshape.1275) | data formatting | bytes 4917248 | tf_op jit(solution)/shard_map/reshape | solution.py:220
  1020.9 8.0 fusion.662
  1043.9 12.9 %copy.1081 = f32[16,4,49,4,49]{4,3,1,2,0:T(4,128)} copy(f32[16,4,49,4,49]{2,1,4,3,0:T(4,128)} %reshape.1276) | data formatting | bytes 4917248 | tf_op jit(solution)/shard_map/reshape | solution.py:220
  1064.2 9.0 fusion.663
  1087.2 12.7 %copy.1083 = f32[16,4,49,4,49]{4,3,1,2,0:T(4,128)} copy(f32[16,4,49,4,49]{2,1,4,3,0:T(4,128)} %reshape.1277) | data formatting | bytes 4917248 | tf_op jit(solution)/shard_map/reshape | solution.py:220
  1100.0 8.0 fusion.664
  1128.7 13.0 %copy.1085 = f32[16,4,49,4,49]{4,3,1,2,0:T(4,128)} copy(f32[16,4,49,4,49]{2,1,4,3,0:T(4,128)} %reshape.1278) | data formatting | bytes 4917248 | tf_op jit(solution)/shard_map/reshape | solution.py:220
  1141.7 8.1 fusion.665
  1155.2 10.5 all-reduce.4
  1171.5 12.7 %all-reduce.2 = (bf16[1,6,128]{2,1,0:T(8,128)(2,1)S(1)}, bf16[1,2,128]{2,1,0:T(2,128)(2,1)S(1)}, bf16[1,512]{1,0:T(2,128)(2,1)S(1)}, bf16[1,169,4]{1,2,0:T(4,128)(2,1)S(1)}) all-reduce(bf16[1,6,128]{2,1,0:T(8,128)(2,1)S(1)} %bitcast.1055, ...), channel_id=1, replica_groups=mesh['section'=2,'fsdp'=4,'replica'=4] {'replica'}, use_global_device_ids=true, to_apply=%region_126.129 | all-reduce | flops 2212 | bytes 8848 | tf_op jit(solution)/shard_map/psum | solution.py:391
  1192.4 9.0 all-gather.20.cloned.1.call-done
  (1183 shorter events, 946.7 us)
Async XLA Ops:
  7.2 66.5 %all-gather.14.cloned.1.call-start = ((), (), s32[]{:S(2)}) async-start(), calls=%async_computation.10 | async-start | bytes 1966080 | tf_op jit(solution)/shard_map/all_gather | solution.py:309
  7.9 96.9 %all-gather.18.cloned.1.call-start = ((), (), s32[]{:S(2)}) async-start(), calls=%async_computation.12 | async-start | bytes 2621440 | tf_op jit(solution)/shard_map/all_gather | solution.py:312
  8.7 96.2 %all-gather.16.cloned.1.call-start = ((), (), s32[]{:S(2)}) async-start(), calls=%async_computation.11 | async-start | bytes 2621440 | tf_op jit(solution)/shard_map/all_gather | solution.py:311
  9.4 1063.7 %reduce-scatter.13.cloned.1.call-start = ((), (), s32[]{:S(2)}) async-start(), calls=%async_computation.7 | async-start | bytes 655360 | tf_op jit(solution)/shard_map/reduce_scatter | solution.py:363
  15.9 256.0 %copy-start.191 = (f32[1,1,512]{2,1,0:T(1,128)}, f32[1,1,512]{2,1,0:T(1,128)S(1)}, u32[]{:S(2)}) copy-start(f32[1,1,512]{2,1,0:T(1,128)S(1)} %get-tuple-element.196) | copy-start | bytes 6148
  15.9 255.9 %copy-start.193 = (f32[1,1,512]{2,1,0:T(1,128)}, f32[1,1,512]{2,1,0:T(1,128)S(1)}, u32[]{:S(2)}) copy-start(f32[1,1,512]{2,1,0:T(1,128)S(1)} %get-tuple-element.197) | copy-start | bytes 6148
  15.9 280.8 %copy-start.202 = (f32[1,1,512]{2,1,0:T(1,128)}, f32[1,1,512]{2,1,0:T(1,128)S(1)}, u32[]{:S(2)}) copy-start(f32[1,1,512]{2,1,0:T(1,128)S(1)} %get-tuple-element.193) | copy-start | bytes 6148
  15.9 280.8 %copy-start.224 = (f32[1,1,512]{2,1,0:T(1,128)}, f32[1,1,512]{2,1,0:T(1,128)S(1)}, u32[]{:S(2)}) copy-start(f32[1,1,512]{2,1,0:T(1,128)S(1)} %get-tuple-element.194) | copy-start | bytes 6148
  15.9 416.2 %copy-start.158 = (f32[1,1,512]{2,1,0:T(1,128)}, f32[1,1,512]{2,1,0:T(1,128)S(1)}, u32[]{:S(2)}) copy-start(f32[1,1,512]{2,1,0:T(1,128)S(1)} %get-tuple-element.198) | copy-start | bytes 6148
  119.3 12.7 %collective-permute-start = (bf16[2,14,14,512]{3,0,2,1:T(2,128)(2,1)}, bf16[2,14,14,512]{3,0,2,1:T(2,128)(2,1)}, u32[]{:S(2)}, u32[]{:S(2)}) collective-permute-start(bf16[2,14,14,512]{3,0,2,1:T(2,128)(2,1)} %get-tuple-element.130), channel_id=1, source_target_pairs={{0,16},{1,17},{2,18},{3,19},{4,20},{5,21},{6,22},{7,23},{8,24},{9,... | collective-permute-start | bytes 1204232 | tf_op jit(solution)/shard_map/ppermute | solution.py:26
  183.3 12.9 %collective-permute-start.1 = (bf16[2,14,14,512]{3,0,2,1:T(2,128)(2,1)}, bf16[2,14,14,512]{3,0,2,1:T(2,128)(2,1)}, u32[]{:S(2)}, u32[]{:S(2)}) collective-permute-start(bf16[2,14,14,512]{3,0,2,1:T(2,128)(2,1)} %get-tuple-element.128), channel_id=1, source_target_pairs={{0,16},{1,17},{2,18},{3,19},{4,20},{5,21},{6,22},{7,23},{8,24},{9,... | collective-permute-start | bytes 1204232 | tf_op jit(solution)/shard_map/ppermute | solution.py:26
  247.3 12.1 collective-permute-start.2
  310.6 12.5 %collective-permute-start.3 = (bf16[2,14,14,512]{3,0,2,1:T(2,128)(2,1)S(1)}, bf16[2,14,14,512]{3,0,2,1:T(2,128)(2,1)S(1)}, u32[]{:S(2)}, u32[]{:S(2)}) collective-permute-start(bf16[2,14,14,512]{3,0,2,1:T(2,128)(2,1)S(1)} %get-tuple-element.124), channel_id=1, source_target_pairs={{0,16},{1,17},{2,18},{3,19},{4,20},{5,21},{6,22},{7,23},{8,24},{9,... | collective-permute-start | bytes 1204232 | tf_op jit(solution)/shard_map/ppermute | solution.py:26
  635.6 40.6 %collective-permute-start.4 = (bf16[2,14,14,512]{3,0,2,1:T(2,128)(2,1)}, bf16[2,14,14,512]{3,0,2,1:T(2,128)(2,1)}, u32[]{:S(2)}, u32[]{:S(2)}) collective-permute-start(bf16[2,14,14,512]{3,0,2,1:T(2,128)(2,1)} %get-tuple-element.113), channel_id=1, source_target_pairs={{16,0},{17,1},{18,2},{19,3},{20,4},{21,5},{22,6},{23,7},{24,8},{25... | collective-permute-start | bytes 1204232 | tf_op jit(solution)/shard_map/ppermute | solution.py:26
  733.2 11.2 collective-permute-start.5
  800.0 9.7 collective-permute-start.6
  864.5 9.9 collective-permute-start.7
  887.9 185.3 %reduce-scatter.15.cloned.1.call-start = ((), (), s32[]{:S(2)}) async-start(), calls=%async_computation.8 | async-start | bytes 2621440 | tf_op jit(solution)/shard_map/reduce_scatter | solution.py:366
  898.5 174.7 %reduce-scatter.17.cloned.1.call-start = ((), (), s32[]{:S(2)}) async-start(), calls=%async_computation.9 | async-start | bytes 2621440 | tf_op jit(solution)/shard_map/reduce_scatter | solution.py:369
  949.2 162.7 %reduce-scatter.11.cloned.1.call-start = ((), (), s32[]{:S(2)}) async-start(), calls=%async_computation.6 | async-start | bytes 1966080 | tf_op jit(solution)/shard_map/reduce_scatter | solution.py:360
  994.1 175.7 %reduce-scatter.19.cloned.1.call-start = ((), (), s32[]{:S(2)}) async-start(), calls=%async_computation.14 | async-start | bytes 163840
  1062.8 107.8 %reduce-scatter.21.cloned.1.call-start = ((), (), s32[]{:S(2)}) async-start(), calls=%async_computation.15 | async-start | bytes 163840
  1063.7 122.8 %all-reduce.7.cloned.1.call-start = ((), (), s32[]{:S(2)}) async-start(), calls=%async_computation.16 | async-start | bytes 2359296 | tf_op jit(solution)/shard_map/psum | solution.py:387
  1073.2 128.2 %all-gather.20.cloned.1.call-start = ((), (), s32[]{:S(2)}) async-start(), calls=%async_computation.13 | async-start | bytes 1966080 | tf_op jit(solution)/shard_map/all_gather | solution.py:20
  (252 other events, 2518.3 us)
Sparse Core Ops, SparseCore 0:
  9.6 22.4 all-gather.13
  33.6 24.0 all-gather.17
  59.2 22.3 all-gather.15
  888.0 20.8 reduce-scatter.12
  911.2 31.1 reduce-scatter.14
  949.3 30.2 reduce-scatter.16
  994.2 27.1 reduce-scatter.10
  1062.9 19.2 reduce-scatter.18
  1084.6 19.6 reduce-scatter.20
  1106.7 56.0 all-reduce.6
  1164.4 36.9 all-gather.19
